TPU v7x, 128 devices: a whole 4x4x4 slice. The times are simulated.
128 devices in a mesh: ha: 16 (over z, y_lo, core), wa: 8 (over x, y_hi).
Axes of the slice: x: 4, y: 4 (y_hi: 2, y_lo: 2; y = y_hi * 2 + y_lo), z: 4, core: 2. Of those that a mesh axis runs over, the one named last changes fastest.
Arguments:
- tokens: bfloat16 [256, 256, 512], P('ha', 'wa'), may hold values from -40 to 40
- cotangent: bfloat16 [256, 256, 512], P('ha', 'wa'), may hold values from -6 to 6
- norm_gain: float32 [512], replicated, may hold values from 0.1 to 1.9
- in_weight: bfloat16 [512, 1536], replicated, may hold values from -0.25 to 0.25
- out_weight: bfloat16 [512, 512], replicated, may hold values from -0.25 to 0.25
- bias_table: float32 [16, 31, 31], replicated, may hold values from -256 to 256
Outputs:
- grad_input: bfloat16 [256, 256, 512], P('ha', 'wa')
- grad_table: float32 [16, 31, 31], replicated
All inputs are finite; a program needn't handle non-finite values.
Results may differ from a plain program's by a relative error of at most 0.011.
Values may be sent and summed in bfloat16 or wider, within the bound.
No kernel may reach another device: no remote copies, remote signals or barrier semaphores. Data moves between devices by JAX's collectives and lax.ppermute only.
A program may use at most 128 MiB of HBM per device.

v0:
```python
import jax
import jax.numpy as jnp
from jax import lax
from jax.sharding import PartitionSpec as P

D = 512
HEADS = 16
HEAD_DIM = 32
WIN = 16
TAB = 31
NORM_EPS = 1e-05


def offset_hot():
    places = jnp.arange(WIN)
    slot_ids = jnp.arange(TAB)
    return (
        places[:, None, None] - places[None, :, None] + (WIN - 1) == slot_ids[None, None, :]
    ).astype(jnp.float32)


def full_bias(bias_table, offset_table):
    partial_rows = jnp.einsum(
        "abd,hde->habe", offset_table, bias_table, precision=lax.Precision.HIGHEST
    )
    spread = jnp.einsum(
        "uve,habe->haubv", offset_table, partial_rows, precision=lax.Precision.HIGHEST
    )
    return spread.reshape(HEADS, WIN * WIN, WIN * WIN)


def group_grad(group_tokens, group_cot, norm_gain, in_weight, out_weight, bias_full, offset_table):
    group_rows = WIN * WIN
    tokens_wide = group_tokens.astype(jnp.float32)
    center = jnp.mean(tokens_wide, axis=-1, keepdims=True)
    shifted = tokens_wide - center
    inv_std = lax.rsqrt(jnp.mean(shifted * shifted, axis=-1, keepdims=True) + NORM_EPS)
    unit_rows = shifted * inv_std
    normed = (unit_rows * norm_gain).astype(jnp.bfloat16)
    mixed_rows = jnp.dot(normed, in_weight, preferred_element_type=jnp.float32)
    query_scale = HEAD_DIM ** (-0.5)
    queries = (
        (mixed_rows[:, :D] * query_scale).astype(jnp.bfloat16).reshape(group_rows, HEADS, HEAD_DIM)
    )
    key_rows = mixed_rows[:, D : 2 * D].astype(jnp.bfloat16).reshape(group_rows, HEADS, HEAD_DIM)
    values = mixed_rows[:, 2 * D :].astype(jnp.bfloat16).reshape(group_rows, HEADS, HEAD_DIM)
    scores = (
        jnp.einsum("thd,shd->hts", queries, key_rows, preferred_element_type=jnp.float32)
        + bias_full
    )
    row_top = jnp.max(scores, axis=-1, keepdims=True)
    exponent = jnp.exp(scores - row_top)
    attn_probs = exponent / jnp.sum(exponent, axis=-1, keepdims=True)
    probs_half = attn_probs.astype(jnp.bfloat16)
    grad_out = lax.dot_general(
        group_cot, out_weight, (((1,), (1,)), ((), ())), preferred_element_type=jnp.float32
    )
    grad_out = grad_out.astype(jnp.bfloat16).reshape(group_rows, HEADS, HEAD_DIM)
    grad_probs = jnp.einsum("thd,shd->hts", grad_out, values, preferred_element_type=jnp.float32)
    grad_values = jnp.einsum(
        "hts,thd->shd", probs_half, grad_out, preferred_element_type=jnp.float32
    ).astype(jnp.bfloat16)
    grad_scores = attn_probs * (
        grad_probs - jnp.sum(attn_probs * grad_probs, axis=-1, keepdims=True)
    )
    scores_half = grad_scores.astype(jnp.bfloat16)
    grad_queries = (
        jnp.einsum("hts,shd->thd", scores_half, key_rows, preferred_element_type=jnp.float32)
        * query_scale
    ).astype(jnp.bfloat16)
    grad_keys = jnp.einsum(
        "hts,thd->shd", scores_half, queries, preferred_element_type=jnp.float32
    ).astype(jnp.bfloat16)
    grad_mixed = jnp.concatenate(
        [
            grad_queries.reshape(group_rows, D),
            grad_keys.reshape(group_rows, D),
            grad_values.reshape(group_rows, D),
        ],
        axis=1,
    )
    grad_normed = lax.dot_general(
        grad_mixed, in_weight, (((1,), (1,)), ((), ())), preferred_element_type=jnp.float32
    )
    grad_unit = grad_normed * norm_gain
    grad_rows = inv_std * (
        grad_unit
        - jnp.mean(grad_unit, axis=-1, keepdims=True)
        - unit_rows * jnp.mean(grad_unit * unit_rows, axis=-1, keepdims=True)
    )
    folded = jnp.einsum(
        "haubv,uve->habe",
        grad_scores.reshape(HEADS, WIN, WIN, WIN, WIN),
        offset_table,
        precision=lax.Precision.HIGHEST,
    )
    table_part = jnp.einsum("habe,abd->hde", folded, offset_table, precision=lax.Precision.HIGHEST)
    return (grad_rows.astype(jnp.bfloat16), table_part)


def body(tokens, cotangent, norm_gain, in_weight, out_weight, bias_table):
    offset_table = offset_hot()
    bias_full = full_bias(bias_table, offset_table)
    high_parts = lax.axis_size("ha")
    wide_parts = lax.axis_size("wa")
    rows_local, cols_local, channels = tokens.shape
    row_steps = WIN // high_parts
    col_steps = WIN // wide_parts
    stride_h = rows_local // row_steps
    stride_w = cols_local // col_steps
    row_groups = stride_h // high_parts
    col_groups = stride_w // wide_parts
    group_count = row_groups * col_groups

    def to_layout(tile_block):
        laid = tile_block.reshape(
            row_steps, high_parts, row_groups, col_steps, wide_parts, col_groups, channels
        )
        laid = laid.transpose(2, 5, 1, 4, 0, 3, 6)
        return laid.reshape(group_count, high_parts, wide_parts, row_steps, col_steps, channels)

    def one_group(pair_rows):
        return group_grad(
            pair_rows[0], pair_rows[1], norm_gain, in_weight, out_weight, bias_full, offset_table
        )

    laid_tokens = to_layout(tokens)
    laid_cot = to_layout(cotangent)

    def swap_rows(laid):
        items = laid.shape[0]
        shaped = laid.reshape(items, high_parts, wide_parts, row_steps, col_steps, channels)
        return shaped.transpose(0, 1, 3, 2, 4, 5).reshape(items, WIN * WIN, channels)

    flat_shape = (group_count, high_parts * wide_parts, row_steps * col_steps, channels)
    grad_rows, table_parts = lax.map(
        one_group,
        (
            swap_rows(
                lax.all_to_all(
                    laid_tokens.reshape(flat_shape),
                    ("ha", "wa"),
                    split_axis=1,
                    concat_axis=1,
                    tiled=True,
                )
            ),
            swap_rows(
                lax.all_to_all(
                    laid_cot.reshape(flat_shape),
                    ("ha", "wa"),
                    split_axis=1,
                    concat_axis=1,
                    tiled=True,
                )
            ),
        ),
    )
    items = grad_rows.shape[0]
    shaped = grad_rows.reshape(items, high_parts, row_steps, wide_parts, col_steps, channels)
    grads_laid, table_parts = (
        shaped.transpose(0, 1, 3, 2, 4, 5).reshape(
            items, high_parts * wide_parts, row_steps * col_steps, channels
        ),
        table_parts,
    )
    returned = lax.all_to_all(grads_laid, ("ha", "wa"), split_axis=1, concat_axis=1, tiled=True)
    returned = returned.reshape(group_count, high_parts, wide_parts, row_steps, col_steps, channels)
    shaped = returned.reshape(
        row_groups, col_groups, high_parts, wide_parts, row_steps, col_steps, channels
    )
    shaped = shaped.transpose(4, 2, 0, 5, 3, 1, 6)
    grad_input = shaped.reshape(rows_local, cols_local, channels)
    grad_table = lax.psum(jnp.sum(table_parts, axis=0), ("ha", "wa"))
    return (grad_input, grad_table)


def solution(mesh):
    in_specs = (P("ha", "wa", None), P("ha", "wa", None), P(), P(), P(), P())
    out_specs = (P("ha", "wa", None), P())
    return jax.shard_map(body, mesh=mesh, in_specs=in_specs, out_specs=out_specs, check_vma=False)
```

profile of v0, /device:TPU:1, one launch (start us, length us, event | category | flops | bytes accessed | tf_op | source)
XLA Modules:
  0.0 330.3 jit_solution(11427729656623690947)
XLA Ops:
  3.5 11.5 %all-to-all-start = ((bf16[2,128,2,512]{3,2,0,1:T(2,128)(2,1)}), bf16[2,128,2,512]{3,2,0,1:T(2,128)(2,1)S(1)}, u32[]{:S(2)}, u32[]{:S(2)}) async-start(bf16[2,128,2,512]{3,2,0,1:T(2,128)(2,1)} %bitcast.1), calls=%async_computation | async-start | bytes 1048576 | tf_op jit(solution)/shard_map/all_to_all | solution.py:140
  19.6 9.5 %all-to-all-done = bf16[2,128,2,512]{3,2,0,1:T(2,128)(2,1)S(1)} async-done(((bf16[2,128,2,512]{3,2,0,1:T(2,128)(2,1)}), bf16[2,128,2,512]{3,2,0,1:T(2,128)(2,1)S(1)}, u32[]{:S(2)}, u32[]{:S(2)}) %all-to-all-start) | async-done | bytes 524320 | tf_op jit(solution)/shard_map/all_to_all | solution.py:140
  29.1 4.7 %all-to-all-start.1 = ((bf16[2,128,2,512]{3,2,0,1:T(2,128)(2,1)}), bf16[2,128,2,512]{3,2,0,1:T(2,128)(2,1)}, u32[]{:S(2)}, u32[]{:S(2)}) async-start(bf16[2,128,2,512]{3,2,0,1:T(2,128)(2,1)} %bitcast.12), calls=%async_computation.1 | async-start | bytes 1048576 | tf_op jit(solution)/shard_map/all_to_all | solution.py:149
  33.8 17.4 %convolution_bitcast_fusion = f32[16,16,16,16,16]{4,3,2,1,0:T(8,128)} fusion(f32[16,16,16,31]{3,1,0,2:T(8,128)S(1)} %fusion.54, s32[16,16]{1,0:T(8,128)S(1)} %copy.74), kind=kOutput, calls=%fused_computation.64 | convolution fusion | flops 390078208 | bytes 4703232 | tf_op jit(solution)/shard_map/uve,habe->haubv/dot_general | solution.py:26
  51.2 23.5 %reshape.83 = f32[16,256,256]{2,1,0:T(8,128)} reshape(f32[16,16,16,16,16]{4,3,2,1,0:T(8,128)} %convolution_bitcast_fusion) | data formatting | bytes 8388608 | tf_op jit(solution)/shard_map/reshape | solution.py:29
  74.7 5.4 %copy.79 = f32[16,256,256]{1,2,0:T(8,128)} copy(f32[16,256,256]{2,1,0:T(8,128)} %reshape.83) | data formatting | bytes 8388608
  83.1 162.9 %while.14 = (s32[]{:T(128)}, bf16[2,256,512]{2,1,0:T(8,128)(2,1)}, f32[2,16,31,31]{2,3,1,0:T(8,128)}, bf16[2,256,512]{2,1,0:T(8,128)(2,1)S(1)}, f32[512]{0:T(512...) while((s32[]{:T(128)}, bf16[2,256,512]{2,1,0:T(8,128)(2,1)}, ...), condition=%wide.region_8.9_spmd.clone.clone, body=%wide.region_0.8_spmd.clone.clone.sunk | while | flops 1734164224 | bytes 137940368 | solution.py:136
  91.3 2.9 convolution_add_fusion.2
  94.3 3.1 fusion.130
  97.5 5.2 %fusion.131 = bf16[16,32,256]{2,1,0:T(8,128)(2,1)} fusion(bf16[256,16,32]{0,2,1:T(8,128)(2,1)S(1)} %bitcast.193, f32[16,256]{1,0:T(8,128)S(1)} %get-tuple-element.273, f32[16,256,256]{1,2,0:T(8,128)} %copy-done.4), kind=kOutput, calls=%fused_computation.13.clone.1 | convolution fusion | flops 70390016 | bytes 4734976 | tf_op jit(solution)/shard_map/while/body/eval_jaxpr/hts,thd->shd/dot_general | solution.py:60
  102.7 3.2 multiply_reduce_fusion.2
  110.5 19.4 %reshape.111 = f32[16,16,16,16,16]{2,1,4,3,0:T(8,128)} reshape(f32[16,256,256]{1,2,0:T(8,128)} %copy-done.2) | data formatting | bytes 8388608 | tf_op jit(solution)/shard_map/while/body/eval_jaxpr/reshape | solution.py:93
  129.9 30.4 %fusion.135 = f32[16,16,16,31,1]{3,1,4,2,0:T(8,128)S(1)} fusion(f32[16,16,16,16,16]{2,1,4,3,0:T(8,128)} %reshape.111, s32[16,16]{0,1:T(8,128)S(1)} %get-tuple-element.314), kind=kOutput, calls=%fused_computation.53.clone.1 | convolution fusion | flops 390086144 | bytes 4703232 | tf_op jit(solution)/shard_map/while/body/eval_jaxpr/haubv,uve->habe/dot_general | solution.py:91
  160.4 3.5 %fusion.136 = f32[2,16,31,31]{2,3,1,0:T(8,128)S(1)} fusion(f32[2,16,31,31]{2,3,1,0:T(8,128)S(1)} %copy-done.13, s32[]{:T(128)S(6)} %copy.114, f32[16,16,16,31,1]{3,1,4,2,0:T(8,128)S(1)} %fusion.135, s32[16,16]{0,1:T(8,128)S(1)} %get-tuple-element.314), kind=kOutput, calls=%fused_computation.18.clone.1 | convolution fusion | flops 47250944 | bytes 2367492 | tf_op jit(solution)/shard_map/while/body/eval_jaxpr/habe,abd->hde/dot_general | solution.py:97
  172.7 2.9 convolution_add_fusion.2
  175.6 3.1 fusion.130
  178.8 5.2 %fusion.131 = bf16[16,32,256]{2,1,0:T(8,128)(2,1)} fusion(bf16[256,16,32]{0,2,1:T(8,128)(2,1)S(1)} %bitcast.193, f32[16,256]{1,0:T(8,128)S(1)} %get-tuple-element.273, f32[16,256,256]{1,2,0:T(8,128)} %copy-done.4), kind=kOutput, calls=%fused_computation.13.clone.1 | convolution fusion | flops 70390016 | bytes 4734976 | tf_op jit(solution)/shard_map/while/body/eval_jaxpr/hts,thd->shd/dot_general | solution.py:60
  184.0 3.2 multiply_reduce_fusion.2
  191.9 19.4 %reshape.111 = f32[16,16,16,16,16]{2,1,4,3,0:T(8,128)} reshape(f32[16,256,256]{1,2,0:T(8,128)} %copy-done.2) | data formatting | bytes 8388608 | tf_op jit(solution)/shard_map/while/body/eval_jaxpr/reshape | solution.py:93
  211.3 30.4 %fusion.135 = f32[16,16,16,31,1]{3,1,4,2,0:T(8,128)S(1)} fusion(f32[16,16,16,16,16]{2,1,4,3,0:T(8,128)} %reshape.111, s32[16,16]{0,1:T(8,128)S(1)} %get-tuple-element.314), kind=kOutput, calls=%fused_computation.53.clone.1 | convolution fusion | flops 390086144 | bytes 4703232 | tf_op jit(solution)/shard_map/while/body/eval_jaxpr/haubv,uve->habe/dot_general | solution.py:91
  241.7 3.5 %fusion.136 = f32[2,16,31,31]{2,3,1,0:T(8,128)S(1)} fusion(f32[2,16,31,31]{2,3,1,0:T(8,128)S(1)} %copy-done.13, s32[]{:T(128)S(6)} %copy.114, f32[16,16,16,31,1]{3,1,4,2,0:T(8,128)S(1)} %fusion.135, s32[16,16]{0,1:T(8,128)S(1)} %get-tuple-element.314), kind=kOutput, calls=%fused_computation.18.clone.1 | convolution fusion | flops 47250944 | bytes 2367492 | tf_op jit(solution)/shard_map/while/body/eval_jaxpr/habe,abd->hde/dot_general | solution.py:97
  246.0 2.4 copy.81
  248.4 9.9 %all-to-all-start.2 = ((bf16[2,128,2,512]{3,0,2,1:T(2,128)(2,1)}), bf16[2,128,2,512]{3,0,2,1:T(2,128)(2,1)S(1)}, u32[]{:S(2)}, u32[]{:S(2)}) async-start(bf16[2,128,2,512]{3,0,2,1:T(2,128)(2,1)} %bitcast.14), calls=%async_computation.2 | async-start | bytes 1048576 | tf_op jit(solution)/shard_map/all_to_all | solution.py:167
  259.4 68.6 %psum.7 = f32[16,31,31]{1,2,0:T(8,128)S(1)} all-reduce(f32[16,31,31]{1,2,0:T(8,128)S(1)} %reduce_sum.63), channel_id=1, replica_groups=mesh['ha'=16,'wa'=8] {'ha','wa'}, use_global_device_ids=true, to_apply=%region_10.11 | all-reduce | flops 15376 | bytes 123008 | tf_op jit(solution)/shard_map/psum | solution.py:174
  (106 shorter events, 40.8 us)
Async XLA Ops:
  0.6 18.0 %copy-start = (f32[16,31,31]{2,0,1:T(8,128)S(1)}, f32[16,31,31]{2,0,1:T(8,128)}, u32[]{:S(2)}) copy-start(f32[16,31,31]{2,0,1:T(8,128)} %param.13) | copy-start | bytes 184516
  3.5 25.5 %all-to-all-start = ((bf16[2,128,2,512]{3,2,0,1:T(2,128)(2,1)}), bf16[2,128,2,512]{3,2,0,1:T(2,128)(2,1)S(1)}, u32[]{:S(2)}, u32[]{:S(2)}) async-start(bf16[2,128,2,512]{3,2,0,1:T(2,128)(2,1)} %bitcast.1), calls=%async_computation | async-start | bytes 1048576 | tf_op jit(solution)/shard_map/all_to_all | solution.py:140
  29.1 22.1 %copy-start.9 = (bf16[2,128,2,512]{3,2,0,1:T(2,128)(2,1)}, bf16[2,128,2,512]{3,2,0,1:T(2,128)(2,1)S(1)}, u32[]{:S(2)}) copy-start(bf16[2,128,2,512]{3,2,0,1:T(2,128)(2,1)S(1)} %all-to-all-done) | copy-start | bytes 1572868
  29.1 51.6 %all-to-all-start.1 = ((bf16[2,128,2,512]{3,2,0,1:T(2,128)(2,1)}), bf16[2,128,2,512]{3,2,0,1:T(2,128)(2,1)}, u32[]{:S(2)}, u32[]{:S(2)}) async-start(bf16[2,128,2,512]{3,2,0,1:T(2,128)(2,1)} %bitcast.12), calls=%async_computation.1 | async-start | bytes 1048576 | tf_op jit(solution)/shard_map/all_to_all | solution.py:149
  74.7 5.4 %copy-start.10 = (bf16[2,128,2,512]{3,2,0,1:T(2,128)(2,1)S(1)}, bf16[2,128,2,512]{3,2,0,1:T(2,128)(2,1)}, u32[]{:S(2)}) copy-start(bf16[2,128,2,512]{3,2,0,1:T(2,128)(2,1)} %copy-done.9) | copy-start | bytes 1572868
  80.1 3.0 copy-start.5
  80.1 3.0 copy-start.6
  80.2 3.0 copy-start.12
  80.2 3.0 copy-start.15
  94.3 3.2 copy-start.4
  94.3 3.2 copy-start.8
  102.7 3.4 %copy-start.3 = (f32[16,256,256]{1,2,0:T(8,128)S(1)}, f32[16,256,256]{1,2,0:T(8,128)}, u32[]{:S(2)}) copy-start(f32[16,256,256]{1,2,0:T(8,128)} %get-tuple-element.274) | copy-start | bytes 12582916 | tf_op jit(solution)/shard_map/while
  106.9 2.0 copy-start.2
  106.9 2.0 copy-start.16
  129.9 30.4 %copy-start.13 = (f32[2,16,31,31]{2,3,1,0:T(8,128)S(1)}, f32[2,16,31,31]{2,3,1,0:T(8,128)}, u32[]{:S(2)}) copy-start(f32[2,16,31,31]{2,3,1,0:T(8,128)} %get-tuple-element.296) | copy-start | bytes 369028 | tf_op jit(solution)/shard_map/while
  129.9 34.7 %copy-start.7 = (bf16[512,512]{1,0:T(8,128)(2,1)S(1)}, bf16[512,512]{1,0:T(8,128)(2,1)}, u32[]{:S(2)}) copy-start(bf16[512,512]{1,0:T(8,128)(2,1)} %get-tuple-element.327) | copy-start | bytes 1572868 | tf_op jit(solution)/shard_map/while
  175.6 3.2 copy-start.4
  175.6 3.2 copy-start.8
  184.0 3.4 %copy-start.3 = (f32[16,256,256]{1,2,0:T(8,128)S(1)}, f32[16,256,256]{1,2,0:T(8,128)}, u32[]{:S(2)}) copy-start(f32[16,256,256]{1,2,0:T(8,128)} %get-tuple-element.274) | copy-start | bytes 12582916 | tf_op jit(solution)/shard_map/while
  188.2 2.0 copy-start.2
  211.3 30.4 %copy-start.13 = (f32[2,16,31,31]{2,3,1,0:T(8,128)S(1)}, f32[2,16,31,31]{2,3,1,0:T(8,128)}, u32[]{:S(2)}) copy-start(f32[2,16,31,31]{2,3,1,0:T(8,128)} %get-tuple-element.296) | copy-start | bytes 369028 | tf_op jit(solution)/shard_map/while
  211.3 34.7 %copy-start.7 = (bf16[512,512]{1,0:T(8,128)(2,1)S(1)}, bf16[512,512]{1,0:T(8,128)(2,1)}, u32[]{:S(2)}) copy-start(bf16[512,512]{1,0:T(8,128)(2,1)} %get-tuple-element.327) | copy-start | bytes 1572868 | tf_op jit(solution)/shard_map/while
  246.0 84.3 %copy-start.1 = (f32[16,31,31]{2,0,1:T(8,128)S(1)}, f32[16,31,31]{2,0,1:T(8,128)}, u32[]{:S(2)}) copy-start(f32[16,31,31]{2,0,1:T(8,128)} %param.13) | copy-start | bytes 184516
  248.4 80.5 %all-to-all-start.2 = ((bf16[2,128,2,512]{3,0,2,1:T(2,128)(2,1)}), bf16[2,128,2,512]{3,0,2,1:T(2,128)(2,1)S(1)}, u32[]{:S(2)}, u32[]{:S(2)}) async-start(bf16[2,128,2,512]{3,0,2,1:T(2,128)(2,1)} %bitcast.14), calls=%async_computation.2 | async-start | bytes 1048576 | tf_op jit(solution)/shard_map/all_to_all | solution.py:167
  (4 other events, 4.1 us)
where the time goes:
time: 332 us; the launch traced here: 330 us
  matrix products  117 us (35%)
  local copies, waits for them, and re-layouts  95.5 us (29%)
  blocking collectives  68.6 us (21%)
  starting transfers between devices  26.1 us (8%)
  other arithmetic  12.9 us (4%)
  waiting for transfers between devices  9.46 us (3%)
    psum x1, blocking collectives, body(): grad_table = lax.psum(jnp.sum(table_parts, axis=0), ('ha', 'wa'))  68.6 us
    dot_general x2, matrix products, group_grad(): jnp.einsum('haubv,uve->habe', grad_scores.reshape(HEADS, WIN, WIN, WIN, W...  60.8 us
    reshape x2, local copies, waits for them, and re-layouts, group_grad(): grad_scores.reshape(HEADS, WIN, WIN, WIN, WIN)  38.8 us
    reshape x1, local copies, waits for them, and re-layouts, full_bias(): return spread.reshape(HEADS, WIN * WIN, WIN * WIN)  23.5 us
    dot_general x1, matrix products, full_bias(): jnp.einsum('uve,habe->haubv', offset_table, partial_rows, precision=lax.P...  17.4 us
    all_to_all x1, starting transfers between devices, body(): lax.all_to_all(laid_tokens.reshape(flat_shape), ('ha', 'wa'), split_axis=...  11.5 us
    dot_general x2, matrix products, group_grad(): jnp.einsum('hts,thd->shd', probs_half, grad_out, preferred_element_type=j...  10.3 us
    all_to_all x1, starting transfers between devices, body(): lax.all_to_all(grads_laid, ('ha', 'wa'), split_axis=1, concat_axis=1, til...  9.89 us
  transfers between devices with their start and end apart: 3, of which 1 were waited for; matrix products, arithmetic and copies ran while one was open for 16% of the time, Pallas kernels for 0%

commit v1 on v0

--- a/solution.py
+++ b/solution.py
@@ -171,7 +171,9 @@
     )
     shaped = shaped.transpose(4, 2, 0, 5, 3, 1, 6)
     grad_input = shaped.reshape(rows_local, cols_local, channels)
-    grad_table = lax.psum(jnp.sum(table_parts, axis=0), ("ha", "wa"))
+    x = jnp.sum(table_parts, axis=0)
+    parts = lax.all_gather(x, ("ha", "wa"), axis=0, tiled=False)
+    grad_table = parts.sum(axis=0)
     return (grad_input, grad_table)
 
 

time: 332 us -> 624 us (1.88)
  waiting for transfers between devices: 9.46 us -> 327 us
  blocking collectives: 68.6 us -> 26.7 us
  between operations: 0.77 us -> 14.2 us
  other arithmetic: 12.9 us -> 25.5 us
  starting transfers between devices: 26.1 us -> 16.2 us
    all_gather x0 -> x1, waiting for transfers between devices: none -> 318 us  [body(): parts = lax.all_gather(x, ('ha', 'wa'), axis=0, tiled=False)]
    psum x1 -> x0, blocking collectives: 68.6 us -> none  [body(): grad_table = lax.psum(jnp.sum(table_parts, axis=0), ('ha', 'wa'))]
    all_to_all x0 -> x1, blocking collectives: none -> 26.7 us  [body(): lax.all_to_all(grads_laid, ('ha', 'wa'), split_axis=1, concat_axis=1, til...]
    reduce_sum x1 -> x2, other arithmetic: 1.13 us -> 13.8 us  [the longest x1 12.7 us: body(): grad_table = parts.sum(axis=0)]
    all_to_all x1 -> x0, starting transfers between devices: 9.89 us -> none  [body(): lax.all_to_all(grads_laid, ('ha', 'wa'), split_axis=1, concat_axis=1, til...]
  transfers between devices with their start and end apart: 3 -> 3, of which waited for: 1 -> 2; matrix products, arithmetic and copies ran while one was open for 16% -> 9% of each run, Pallas kernels for 0% -> 0%
where the time goes in v1:
time: 624 us; the launch traced here: 621 us
  waiting for transfers between devices  327 us (52%)
  matrix products  117 us (19%)
  local copies, waits for them, and re-layouts  94.7 us (15%)
  blocking collectives  26.7 us (4%)
  other arithmetic  25.5 us (4%)
  starting transfers between devices  16.2 us (3%)
  between operations  14.2 us (2%)
    all_gather x1, waiting for transfers between devices, body(): parts = lax.all_gather(x, ('ha', 'wa'), axis=0, tiled=False)  318 us
    dot_general x2, matrix products, group_grad(): jnp.einsum('haubv,uve->habe', grad_scores.reshape(HEADS, WIN, WIN, WIN, W...  60.8 us
    reshape x2, local copies, waits for them, and re-layouts, group_grad(): grad_scores.reshape(HEADS, WIN, WIN, WIN, WIN)  38.8 us
    all_to_all x1, blocking collectives, body(): lax.all_to_all(grads_laid, ('ha', 'wa'), split_axis=1, concat_axis=1, til...  26.7 us
    reshape x1, local copies, waits for them, and re-layouts, full_bias(): return spread.reshape(HEADS, WIN * WIN, WIN * WIN)  23.5 us
    dot_general x1, matrix products, full_bias(): jnp.einsum('uve,habe->haubv', offset_table, partial_rows, precision=lax.P...  17.4 us
    reduce_sum x1, other arithmetic, body(): grad_table = parts.sum(axis=0)  12.7 us
  transfers between devices with their start and end apart: 3, of which 2 were waited for; matrix products, arithmetic and copies ran while one was open for 9% of the time, Pallas kernels for 0%

profile of v1, /device:TPU:1, one launch (start us, length us, event | category | flops | bytes accessed | tf_op | source)
XLA Modules:
  0.0 621.3 jit_solution(7422559573053347119)
XLA Ops:
  10.1 11.5 %all-to-all-start = ((bf16[2,128,2,512]{3,2,0,1:T(2,128)(2,1)}), bf16[2,128,2,512]{3,2,0,1:T(2,128)(2,1)S(1)}, u32[]{:S(2)}, u32[]{:S(2)}) async-start(bf16[2,128,2,512]{3,2,0,1:T(2,128)(2,1)} %bitcast.1), calls=%async_computation | async-start | bytes 1048576 | tf_op jit(solution)/shard_map/all_to_all | solution.py:140
  26.2 9.4 %all-to-all-done = bf16[2,128,2,512]{3,2,0,1:T(2,128)(2,1)S(1)} async-done(((bf16[2,128,2,512]{3,2,0,1:T(2,128)(2,1)}), bf16[2,128,2,512]{3,2,0,1:T(2,128)(2,1)S(1)}, u32[]{:S(2)}, u32[]{:S(2)}) %all-to-all-start) | async-done | bytes 524320 | tf_op jit(solution)/shard_map/all_to_all | solution.py:140
  35.6 4.7 all-to-all-start.1
  40.4 17.4 %convolution_bitcast_fusion = f32[16,16,16,16,16]{4,3,2,1,0:T(8,128)} fusion(f32[16,16,16,31]{3,1,0,2:T(8,128)S(1)} %fusion.54, s32[16,16]{1,0:T(8,128)S(1)} %copy.74), kind=kOutput, calls=%fused_computation.64 | convolution fusion | flops 390078208 | bytes 4703232 | tf_op jit(solution)/shard_map/uve,habe->haubv/dot_general | solution.py:26
  57.8 23.5 %reshape.83 = f32[16,256,256]{2,1,0:T(8,128)} reshape(f32[16,16,16,16,16]{4,3,2,1,0:T(8,128)} %convolution_bitcast_fusion) | data formatting | bytes 8388608 | tf_op jit(solution)/shard_map/reshape | solution.py:29
  81.3 5.4 copy.79
  89.7 162.8 %while.14 = (s32[]{:T(128)}, bf16[2,256,512]{2,1,0:T(8,128)(2,1)}, f32[2,16,31,31]{2,3,1,0:T(8,128)}, bf16[2,256,512]{2,1,0:T(8,128)(2,1)S(1)}, f32[512]{0:T(512...) while((s32[]{:T(128)}, bf16[2,256,512]{2,1,0:T(8,128)(2,1)}, ...), condition=%wide.region_8.9_spmd.clone.clone, body=%wide.region_0.8_spmd.clone.clone.sunk | while | flops 1734164224 | bytes 137940368 | solution.py:136
  97.9 2.9 convolution_add_fusion.2
  100.9 3.1 fusion.130
  104.1 5.2 fusion.131
  109.2 3.2 multiply_reduce_fusion.2
  117.1 19.4 %reshape.112 = f32[16,16,16,16,16]{2,1,4,3,0:T(8,128)} reshape(f32[16,256,256]{1,2,0:T(8,128)} %copy-done.2) | data formatting | bytes 8388608 | tf_op jit(solution)/shard_map/while/body/eval_jaxpr/reshape | solution.py:93
  136.5 30.4 %fusion.135 = f32[16,16,16,31,1]{3,1,4,2,0:T(8,128)S(1)} fusion(f32[16,16,16,16,16]{2,1,4,3,0:T(8,128)} %reshape.112, s32[16,16]{0,1:T(8,128)S(1)} %get-tuple-element.314), kind=kOutput, calls=%fused_computation.53.clone.1 | convolution fusion | flops 390086144 | bytes 4703232 | tf_op jit(solution)/shard_map/while/body/eval_jaxpr/haubv,uve->habe/dot_general | solution.py:91
  166.9 3.5 fusion.136
  179.2 2.9 convolution_add_fusion.2
  182.2 3.1 fusion.130
  185.4 5.2 fusion.131
  190.6 3.2 multiply_reduce_fusion.2
  198.4 19.4 %reshape.112 = f32[16,16,16,16,16]{2,1,4,3,0:T(8,128)} reshape(f32[16,256,256]{1,2,0:T(8,128)} %copy-done.2) | data formatting | bytes 8388608 | tf_op jit(solution)/shard_map/while/body/eval_jaxpr/reshape | solution.py:93
  217.8 30.4 %fusion.135 = f32[16,16,16,31,1]{3,1,4,2,0:T(8,128)S(1)} fusion(f32[16,16,16,16,16]{2,1,4,3,0:T(8,128)} %reshape.112, s32[16,16]{0,1:T(8,128)S(1)} %get-tuple-element.314), kind=kOutput, calls=%fused_computation.53.clone.1 | convolution fusion | flops 390086144 | bytes 4703232 | tf_op jit(solution)/shard_map/while/body/eval_jaxpr/haubv,uve->habe/dot_general | solution.py:91
  248.3 3.5 fusion.136
  256.2 26.7 %all_to_all.15 = bf16[2,128,2,512]{3,0,2,1:T(2,128)(2,1)S(1)} all-to-all(bf16[2,128,2,512]{3,0,2,1:T(2,128)(2,1)S(1)} %bitcast.200), channel_id=1, replica_groups=mesh['ha'=16,'wa'=8] {'ha','wa'}, dimensions={1} | all-to-all | bytes 1048576 | tf_op jit(solution)/shard_map/all_to_all | solution.py:167
  284.3 317.5 %all-gather.3.cloned.1.call-done = f32[2048,31,31]{2,0,1:T(8,128)} async-done(((f32[16,31,31]{2,0,1:T(8,128)}), f32[2048,31,31]{2,0,1:T(8,128)}) %all-gather.3.cloned.1.call-update) | async-done | bytes 7872528 | tf_op jit(solution)/shard_map/all_gather | solution.py:175
  601.8 12.7 %reduce_sum.73 = f32[16,31,31]{2,0,1:T(8,128)} reduce(f32[128,16,31,31]{3,1,0,2:T(8,128)} %bitcast.192, f32[]{:T(128)} %constant.34.clone.1), dimensions={0}, to_apply=%region_10.11 | reduce | flops 1952752 | bytes 7934020 | tf_op jit(solution)/shard_map/reduce_sum | solution.py:176
  (108 shorter events, 42.5 us)
Async XLA Ops:
  7.2 18.0 %copy-start = (f32[16,31,31]{2,0,1:T(8,128)S(1)}, f32[16,31,31]{2,0,1:T(8,128)}, u32[]{:S(2)}) copy-start(f32[16,31,31]{2,0,1:T(8,128)} %param.13) | copy-start | bytes 184516
  10.1 25.5 %all-to-all-start = ((bf16[2,128,2,512]{3,2,0,1:T(2,128)(2,1)}), bf16[2,128,2,512]{3,2,0,1:T(2,128)(2,1)S(1)}, u32[]{:S(2)}, u32[]{:S(2)}) async-start(bf16[2,128,2,512]{3,2,0,1:T(2,128)(2,1)} %bitcast.1), calls=%async_computation | async-start | bytes 1048576 | tf_op jit(solution)/shard_map/all_to_all | solution.py:140
  35.6 22.2 %copy-start.9 = (bf16[2,128,2,512]{3,2,0,1:T(2,128)(2,1)}, bf16[2,128,2,512]{3,2,0,1:T(2,128)(2,1)S(1)}, u32[]{:S(2)}) copy-start(bf16[2,128,2,512]{3,2,0,1:T(2,128)(2,1)S(1)} %all-to-all-done) | copy-start | bytes 1572868
  35.6 51.6 %all-to-all-start.1 = ((bf16[2,128,2,512]{3,2,0,1:T(2,128)(2,1)}), bf16[2,128,2,512]{3,2,0,1:T(2,128)(2,1)}, u32[]{:S(2)}, u32[]{:S(2)}) async-start(bf16[2,128,2,512]{3,2,0,1:T(2,128)(2,1)} %bitcast.12), calls=%async_computation.1 | async-start | bytes 1048576 | tf_op jit(solution)/shard_map/all_to_all | solution.py:149
  40.3 561.5 %all-gather.3.cloned.1.call-start = ((), (), s32[]{:S(2)}) async-start(), calls=%async_computation.3 | async-start | bytes 32759808 | tf_op jit(solution)/shard_map/all_gather | solution.py:175
  81.3 5.4 copy-start.10
  86.7 3.0 copy-start.5
  86.7 3.0 copy-start.6
  86.7 3.0 copy-start.12
  86.7 3.0 copy-start.15
  100.9 3.2 copy-start.4
  100.9 3.2 copy-start.8
  109.2 3.4 copy-start.3
  113.5 2.0 copy-start.2
  136.5 30.4 %copy-start.13 = (f32[2,16,31,31]{2,3,1,0:T(8,128)S(1)}, f32[2,16,31,31]{2,3,1,0:T(8,128)}, u32[]{:S(2)}) copy-start(f32[2,16,31,31]{2,3,1,0:T(8,128)} %get-tuple-element.296) | copy-start | bytes 369028 | tf_op jit(solution)/shard_map/while
  136.5 34.7 %copy-start.7 = (bf16[512,512]{1,0:T(8,128)(2,1)S(1)}, bf16[512,512]{1,0:T(8,128)(2,1)}, u32[]{:S(2)}) copy-start(bf16[512,512]{1,0:T(8,128)(2,1)} %get-tuple-element.329) | copy-start | bytes 1572868 | tf_op jit(solution)/shard_map/while
  182.2 3.2 copy-start.4
  182.2 3.2 copy-start.8
  190.6 3.4 copy-start.3
  194.8 2.0 copy-start.2
  194.8 1.9 copy-start.16
  217.8 30.4 %copy-start.13 = (f32[2,16,31,31]{2,3,1,0:T(8,128)S(1)}, f32[2,16,31,31]{2,3,1,0:T(8,128)}, u32[]{:S(2)}) copy-start(f32[2,16,31,31]{2,3,1,0:T(8,128)} %get-tuple-element.296) | copy-start | bytes 369028 | tf_op jit(solution)/shard_map/while
  217.8 34.7 %copy-start.7 = (bf16[512,512]{1,0:T(8,128)(2,1)S(1)}, bf16[512,512]{1,0:T(8,128)(2,1)}, u32[]{:S(2)}) copy-start(bf16[512,512]{1,0:T(8,128)(2,1)} %get-tuple-element.329) | copy-start | bytes 1572868 | tf_op jit(solution)/shard_map/while
  601.8 12.7 %copy-start.1 = (f32[16,31,31]{2,0,1:T(8,128)S(1)}, f32[16,31,31]{2,0,1:T(8,128)}, u32[]{:S(2)}) copy-start(f32[16,31,31]{2,0,1:T(8,128)} %param.13) | copy-start | bytes 184516
  (4 other events, 4.1 us)
Sparse Core Ops, SparseCore 0:
  254.7 347.0 all-gather.2
